TPU v7x, 32 devices: a whole 2x2x4 slice. The times are simulated.
32 devices in a mesh: seq: 8 (over y, x, core), exp: 4 (over z).
Axes of the slice: x: 2, y: 2, z: 4, core: 2. Of those that a mesh axis runs over, the one named last changes fastest.
Arguments:
- layer_input: bfloat16 [4, 4096, 768], P('exp', 'seq'), may hold values from -6 to 6
- token_ids: int32 [4, 4096], P('exp', 'seq'), may hold values from 0 to 8007, as said below
- segment_ids: int32 [4, 4096], P('exp'), may hold values from 0 to 7, never falling along the last dimension, each value on 1 to 1024 neighbouring positions
- hash_table: int32 [8008], replicated, may hold values from 0 to 3, as said below
- first_gain: float32 [768], replicated, may hold values from 0.25 to 1.75
- first_bias: float32 [768], replicated, may hold values from -1.5 to 1.5
- second_gain: float32 [768], replicated, may hold values from 0.25 to 1.75
- second_bias: float32 [768], replicated, may hold values from -1.5 to 1.5
- w_qkv: bfloat16 [768, 2304], replicated, may hold values from -0.21875 to 0.21875
- w_out: bfloat16 [768, 768], replicated, may hold values from -3 to 3
- w_up: bfloat16 [4, 768, 3072], P('exp'), may hold values from -0.21875 to 0.21875
- w_down: bfloat16 [4, 3072, 768], P('exp'), may hold values from -0.109375 to 0.109375
- cotangent: bfloat16 [4, 4096, 768], P('exp', 'seq'), may hold values from -6 to 6
Outputs:
- layer_output: bfloat16 [4, 4096, 768], P('exp', 'seq')
- grad_input: float32 [4, 4096, 768], P('exp', 'seq')
- grad_w_qkv: float32 [768, 2304], replicated
- grad_w_out: float32 [768, 768], replicated
- grad_first_gain: float32 [768], replicated
- grad_first_bias: float32 [768], replicated
- grad_second_gain: float32 [768], replicated
- grad_second_bias: float32 [768], replicated
- grad_w_up: float32 [4, 768, 3072], P('exp')
- grad_w_down: float32 [4, 3072, 768], P('exp')
Inputs may be any that keep to these rules, and one draw needn't show every extreme that they name: `token_ids`: token ids range over the vocabulary. Among the 512 positions that one device holds, hash_table sends exactly 256 to one expert, the same expert on all devices that hold the same positions of their sequences, and the other experts' counts differ from one another by at most one. `hash_table`: every expert is named by 2002 token ids. `segment_ids`: numbers never fall along a sequence; each document holds 1 to 1024 neighbouring positions, and one in every sequence holds exactly 1024.
All inputs are finite; a program needn't handle non-finite values.
Results may differ from a plain program's by a relative error of at most 0.017.
Values may be sent and summed in bfloat16 or wider, within the bound.
No kernel may reach another device: no remote copies, remote signals or barrier semaphores. Data moves between devices by JAX's collectives and lax.ppermute only.
A program may use at most 192 MiB of HBM per device.

v0:
```python
import math
import jax
import jax.numpy as jnp
from jax import lax
from jax.sharding import PartitionSpec as P

HEADS = 12
HEAD_DIM = 64
DOC_MOST = 1024
NEG_BIG = -1e30
EPSILON = 1e-05


def passed_along(block, axis, distance):
    devices = range(lax.axis_size(axis))
    route = [(i - distance, i) for i in devices if i - distance in devices]
    return lax.ppermute(block, axis, route)


def smooth_gate(values):
    return jax.nn.gelu(values, approximate=True)


def norm_rows(values):
    center = values - jnp.mean(values, axis=-1, keepdims=True)
    scale = lax.rsqrt(jnp.mean(center * center, axis=-1, keepdims=True) + EPSILON)
    return (center * scale, scale)


def norm_back(grad_normed, normed, scale):
    inner = jnp.mean(grad_normed * normed, axis=-1, keepdims=True)
    return scale * (grad_normed - jnp.mean(grad_normed, axis=-1, keepdims=True) - normed * inner)


def over_blocks(step, state, pieces, first):
    length = pieces[0].shape[0]
    stride = math.gcd(length, 512)

    def advance(index, current):
        begin = index * stride
        parts = tuple((piece for piece in pieces))
        return step(current, parts, first + begin)

    return lax.fori_loop(0, length // stride, advance, state)


def allowed_pairs(query_pos, query_seg, key_pos, key_seg, limit):
    inside = (key_pos[None, :] >= 0) & (query_pos[:, None] < limit)
    return (
        inside & (key_pos[None, :] <= query_pos[:, None]) & (key_seg[None, :] == query_seg[:, None])
    )


def head_split(rows):
    return rows.reshape(rows.shape[0], HEADS, HEAD_DIM)


def forward_step(queries, query_pos, query_seg, segment_row, limit):
    width = HEADS * HEAD_DIM
    scale = HEAD_DIM ** (-0.5)

    def step(state, parts, first):
        run_max, run_total, weighted = state
        count = parts[0].shape[0]
        key_rows = head_split(parts[0][:, :width])
        value_rows = head_split(parts[0][:, width:])
        key_pos = first + jnp.arange(count, dtype=jnp.int32)
        key_seg = lax.dynamic_slice_in_dim(segment_row, first, count, 0)
        allowed = allowed_pairs(query_pos, query_seg, key_pos, key_seg, limit)[None]
        scores = (
            jnp.einsum("qhd,khd->hqk", queries, key_rows, preferred_element_type=jnp.float32)
            * scale
        )
        new_max = jnp.maximum(run_max, jnp.max(jnp.where(allowed, scores, NEG_BIG), axis=-1))
        shares = jnp.where(allowed, jnp.exp(scores - new_max[..., None]), 0.0)
        factor = jnp.exp(run_max - new_max)
        run_total = run_total * factor + jnp.sum(shares, axis=-1)
        update = jnp.einsum(
            "hqk,khd->qhd",
            shares.astype(jnp.bfloat16),
            value_rows,
            preferred_element_type=jnp.float32,
        )
        weighted = weighted * factor.T[:, :, None] + update
        return (new_max, run_total, weighted)

    return step


def backward_core(queries, grad_heads, log_total, delta, key_rows, value_rows, allowed):
    scale = HEAD_DIM ** (-0.5)
    scores = (
        jnp.einsum("qhd,khd->hqk", queries, key_rows, preferred_element_type=jnp.float32) * scale
    )
    soft = jnp.where(allowed[None], jnp.exp(scores - log_total[..., None]), 0.0)
    grad_soft = jnp.einsum(
        "qhd,khd->hqk", grad_heads, value_rows, preferred_element_type=jnp.float32
    )
    grad_scores = (soft * (grad_soft - delta[..., None])).astype(jnp.bfloat16)
    return (soft.astype(jnp.bfloat16), grad_scores)


def query_step(queries, grad_heads, log_total, delta, query_pos, query_seg, segment_row, limit):
    width = HEADS * HEAD_DIM
    scale = HEAD_DIM ** (-0.5)

    def step(state, parts, first):
        count = parts[0].shape[0]
        key_rows = head_split(parts[0][:, :width])
        value_rows = head_split(parts[0][:, width:])
        key_pos = first + jnp.arange(count, dtype=jnp.int32)
        key_seg = lax.dynamic_slice_in_dim(segment_row, first, count, 0)
        allowed = allowed_pairs(query_pos, query_seg, key_pos, key_seg, limit)
        soft_low, grad_scores = backward_core(
            queries, grad_heads, log_total, delta, key_rows, value_rows, allowed
        )
        grad_query = (
            jnp.einsum("hqk,khd->qhd", grad_scores, key_rows, preferred_element_type=jnp.float32)
            * scale
        )
        grad_q, grad_block = state
        grad_keys = (
            jnp.einsum("hqk,qhd->khd", grad_scores, queries, preferred_element_type=jnp.float32)
            * scale
        )
        grad_values = jnp.einsum(
            "hqk,qhd->khd", soft_low, grad_heads, preferred_element_type=jnp.float32
        )
        joined = jnp.concatenate(
            [grad_keys.reshape(count, width), grad_values.reshape(count, width)], axis=1
        )
        current = grad_block
        grad_block = current + joined
        return (grad_q + grad_query, grad_block)

    return step


def on_device(
    layer_input,
    token_ids,
    segment_ids,
    hash_table,
    first_gain,
    first_bias,
    second_gain,
    second_bias,
    w_qkv,
    w_out,
    w_up,
    w_down,
    cotangent,
):
    local_len = layer_input.shape[1]
    width = layer_input.shape[2]
    sources = lax.axis_size("exp")
    local_exp = w_up.shape[0]
    experts_total = local_exp * sources
    capacity = 2 * local_len // experts_total
    total_len = local_len * lax.axis_size("seq")
    reach_blocks = (DOC_MOST + local_len - 2) // local_len
    offset = lax.axis_index("seq") * local_len
    segment_row = segment_ids[0]
    query_pos = offset + jnp.arange(local_len, dtype=jnp.int32)
    query_seg = lax.dynamic_slice_in_dim(segment_row, offset, local_len, 0)
    inputs = layer_input[0].astype(jnp.float32)
    normed_one, scale_one = norm_rows(inputs)
    attn_in = (normed_one * first_gain + first_bias).astype(jnp.bfloat16)
    projected = jnp.dot(attn_in, w_qkv, preferred_element_type=jnp.float32).astype(jnp.bfloat16)
    queries = head_split(projected[:, :width])
    key_value = projected[:, width:]
    kv_blocks = [key_value]
    moving = key_value
    for hop_index in range(reach_blocks):
        moving = passed_along(moving, "seq", 1)
        kv_blocks.append(moving)
    state = (
        jnp.full((HEADS, local_len), NEG_BIG, jnp.float32),
        jnp.zeros((HEADS, local_len), jnp.float32),
        jnp.zeros((local_len, HEADS, HEAD_DIM), jnp.float32),
    )
    attend = forward_step(queries, query_pos, query_seg, segment_row, total_len)
    for block_index in range(reach_blocks + 1):
        state = over_blocks(
            attend, state, (kv_blocks[block_index],), offset - block_index * local_len
        )
    run_max, run_total, weighted = state
    attn_exact = (weighted / run_total.T[:, :, None]).reshape(local_len, width)
    log_total = run_max + jnp.log(run_total)
    attn_rows = attn_exact.astype(jnp.bfloat16)
    resid = inputs + jnp.dot(attn_rows, w_out, preferred_element_type=jnp.float32)
    normed_two, scale_two = norm_rows(resid)
    ffn_in = (normed_two * second_gain + second_bias).astype(jnp.bfloat16)
    choice_ids = hash_table[token_ids[0]]
    order = jnp.argsort(choice_ids, stable=True)
    places = jnp.argsort(order, stable=True)
    expert_grid = jnp.arange(experts_total, dtype=jnp.int32)
    matches = choice_ids[:, None] == expert_grid[None, :]
    counts = jnp.sum(matches.astype(jnp.int32), axis=0)
    starts = jnp.cumsum(counts) - counts
    slot_grid = jnp.arange(capacity, dtype=jnp.int32)
    gather_index = order[jnp.minimum(starts[:, None] + slot_grid[None, :], local_len - 1)]
    filled = (slot_grid[None, :] < counts[:, None])[:, :, None]
    own_start = jnp.sum(jnp.where(matches, starts[None, :], 0), axis=1)
    token_slot = choice_ids * capacity + places - own_start
    send = jnp.where(filled, ffn_in[gather_index], jnp.zeros((), jnp.bfloat16))
    received = lax.all_to_all(send, "exp", split_axis=0, concat_axis=0, tiled=True)
    grouped = received.reshape(sources, local_exp, capacity, width)
    pre_act = jnp.einsum("secd,edf->secf", grouped, w_up, preferred_element_type=jnp.float32)
    activated, gate_pullback = jax.vjp(smooth_gate, pre_act)
    hidden = activated.astype(jnp.bfloat16)
    expert_out = jnp.einsum(
        "secf,efd->secd", hidden, w_down, preferred_element_type=jnp.float32
    ).astype(jnp.bfloat16)
    returned = lax.all_to_all(
        expert_out.reshape(experts_total, capacity, width),
        "exp",
        split_axis=0,
        concat_axis=0,
        tiled=True,
    )
    ffn_rows = returned.reshape(experts_total * capacity, width)[token_slot].astype(jnp.float32)
    layer_output = (resid + ffn_rows).astype(jnp.bfloat16)
    grad_final = cotangent[0].astype(jnp.float32)
    grad_branch = grad_final.astype(jnp.bfloat16)
    grad_send = jnp.where(filled, grad_branch[gather_index], jnp.zeros((), jnp.bfloat16))
    grad_received = lax.all_to_all(
        grad_send, "exp", split_axis=0, concat_axis=0, tiled=True
    ).reshape(sources, local_exp, capacity, width)
    grad_w_down = jnp.einsum(
        "secf,secd->efd", hidden, grad_received, preferred_element_type=jnp.float32
    )
    grad_hidden = jnp.einsum(
        "secd,efd->secf", grad_received, w_down, preferred_element_type=jnp.float32
    )
    grad_pre = gate_pullback(grad_hidden)[0].astype(jnp.bfloat16)
    grad_w_up = jnp.einsum("secd,secf->edf", grouped, grad_pre, preferred_element_type=jnp.float32)
    grad_slots = jnp.einsum(
        "secf,edf->secd", grad_pre, w_up, preferred_element_type=jnp.float32
    ).astype(jnp.bfloat16)
    grad_back = lax.all_to_all(
        grad_slots.reshape(experts_total, capacity, width),
        "exp",
        split_axis=0,
        concat_axis=0,
        tiled=True,
    )
    grad_ffn_in = grad_back.reshape(experts_total * capacity, width)[token_slot].astype(jnp.float32)
    grad_second_gain = jnp.sum(grad_ffn_in * normed_two, axis=0)
    grad_second_bias = jnp.sum(grad_ffn_in, axis=0)
    grad_resid = grad_final + norm_back(grad_ffn_in * second_gain, normed_two, scale_two)
    grad_attn = grad_resid.astype(jnp.bfloat16)
    grad_w_out = jnp.einsum("cd,ce->de", attn_rows, grad_attn, preferred_element_type=jnp.float32)
    grad_out_rows = jnp.einsum(
        "ce,de->cd", grad_attn, w_out, preferred_element_type=jnp.float32
    ).astype(jnp.bfloat16)
    grad_heads = head_split(grad_out_rows)
    delta = jnp.sum(grad_heads.astype(jnp.float32) * head_split(attn_exact), axis=-1).T
    back_blocks = [key_value]
    moving = key_value
    for hop_index in range(reach_blocks):
        moving = passed_along(moving, "seq", 1)
        back_blocks.append(moving)
    grad_query = jnp.zeros((local_len, HEADS, HEAD_DIM), jnp.float32)
    block_grads = []
    for block_index in range(reach_blocks + 1):
        base = offset - block_index * local_len
        back_step = query_step(
            queries, grad_heads, log_total, delta, query_pos, query_seg, segment_row, total_len
        )
        grad_query, grad_block = over_blocks(
            back_step,
            (grad_query, jnp.zeros((local_len, 2 * width), jnp.float32)),
            (back_blocks[block_index],),
            base,
        )
        block_grads.append(grad_block)
    carried = block_grads[reach_blocks]
    for block_index in range(reach_blocks, 0, -1):
        carried = (
            passed_along(carried.astype(jnp.bfloat16), "seq", -1).astype(carried.dtype)
            + block_grads[block_index - 1]
        )
    grad_proj = jnp.concatenate([grad_query.reshape(local_len, width), carried], axis=1).astype(
        jnp.bfloat16
    )
    grad_w_qkv = jnp.einsum("cd,ce->de", attn_in, grad_proj, preferred_element_type=jnp.float32)
    grad_attn_in = jnp.einsum("ce,de->cd", grad_proj, w_qkv, preferred_element_type=jnp.float32)
    grad_first_gain = jnp.sum(grad_attn_in * normed_one, axis=0)
    grad_first_bias = jnp.sum(grad_attn_in, axis=0)
    grad_input = grad_resid + norm_back(grad_attn_in * first_gain, normed_one, scale_one)
    dense = lax.psum(
        (
            grad_w_qkv,
            grad_w_out,
            grad_first_gain,
            grad_first_bias,
            grad_second_gain,
            grad_second_bias,
        ),
        ("seq", "exp"),
    )
    expert_sums = (
        lax.psum(grad_w_up.astype(jnp.bfloat16), "seq").astype(jnp.float32),
        lax.psum(grad_w_down.astype(jnp.bfloat16), "seq").astype(jnp.float32),
    )
    return (
        layer_output[None],
        grad_input[None],
        dense[0],
        dense[1],
        dense[2],
        dense[3],
        dense[4],
        dense[5],
        expert_sums[0],
        expert_sums[1],
    )


def solution(mesh):
    in_specs = (
        P("exp", "seq", None),
        P("exp", "seq"),
        P("exp", None),
        P(),
        P(),
        P(),
        P(),
        P(),
        P(),
        P(),
        P("exp", None, None),
        P("exp", None, None),
        P("exp", "seq", None),
    )
    out_specs = (
        P("exp", "seq", None),
        P("exp", "seq", None),
        P(),
        P(),
        P(),
        P(),
        P(),
        P(),
        P("exp", None, None),
        P("exp", None, None),
    )
    return jax.shard_map(
        on_device, mesh=mesh, in_specs=in_specs, out_specs=out_specs, check_vma=False
    )
```

profile of v0, /device:TPU:0, one launch (start us, length us, event | category | flops | bytes accessed | tf_op | source)
XLA Modules:
  0.0 691.7 jit_solution(2766946564341442537)
XLA Ops:
  27.7 11.3 %gather_fusion.1 = s32[1024]{0:T(1024)} fusion(s32[512]{0:T(512)S(1)} %get-tuple-element.163, s32[1024]{0:T(1024)S(1)} %broadcast_clamp_fusion.1), kind=kCustom, calls=%fused_computation.1 | custom fusion | bytes 12288 | tf_op jit(solution)/shard_map/gather | solution.py:202
  58.6 7.0 %gather_fusion.4 = bf16[1024,768]{1,0:T(8,128)(2,1)} fusion(bf16[512,768]{1,0:T(8,128)(2,1)} %bitcast.289, s32[1024]{0:T(1024)S(1)} %broadcast_clamp_fusion), kind=kCustom, calls=%fused_computation.4 | custom fusion | bytes 3149824 | tf_op jit(solution)/shard_map/gather | solution.py:226
  65.6 8.6 %select_reduce_fusion.2 = (f32[12,512]{1,0:T(8,128)}, f32[12,512,512]{1,2,0:T(8,128)}) fusion(pred[512,512]{0,1:T(8,128)(4,1)} %get-tuple-element.239, bf16[512,12,64]{0,2,1:T(8,128)(2,1)} %bitcast.294, bf16[512,12,64]{0,2,1:T(8,128)(2,1)} %bitcast.302), kind=kOutput, calls=%fused_computation.33 | convolution fusion | flops 412084224 | bytes 14442496 | tf_op jit(solution)/shard_map/while/body/eval_jaxpr/qhd,khd->hqk/dot_general | solution.py:71
  81.5 8.6 %select_reduce_fusion.1 = (f32[12,512]{1,0:T(8,128)}, f32[12,512,512]{1,2,0:T(8,128)}) fusion(pred[512,512]{0,1:T(8,128)(4,1)} %get-tuple-element.241, bf16[512,12,64]{0,2,1:T(8,128)(2,1)} %bitcast.295, bf16[512,12,64]{0,2,1:T(8,128)(2,1)} %bitcast.300), kind=kOutput, calls=%fused_computation.31 | convolution fusion | flops 412084224 | bytes 14442496 | tf_op jit(solution)/shard_map/while/body/eval_jaxpr/qhd,khd->hqk/dot_general | solution.py:71
  97.3 8.1 %select_reduce_fusion = (f32[12,512]{1,0:T(8,128)S(1)}, f32[12,512,512]{1,2,0:T(8,128)}) fusion(pred[512,512]{0,1:T(8,128)(4,1)} %get-tuple-element.240, bf16[512,12,64]{0,2,1:T(8,128)(2,1)} %bitcast.296, bf16[512,12,64]{0,2,1:T(8,128)(2,1)} %bitcast.304), kind=kOutput, calls=%fused_computation.29 | convolution fusion | flops 412084224 | bytes 14442496 | tf_op jit(solution)/shard_map/while/body/eval_jaxpr/qhd,khd->hqk/dot_general | solution.py:71
  106.1 7.3 %fusion.13 = f32[12,512]{1,0:T(8,128)S(1)} fusion(f32[12,512,512]{1,2,0:T(8,128)} %get-tuple-element.247, f32[12,512]{1,0:T(8,128)S(1)} %get-tuple-element.210, pred[512,512]{0,1:T(8,128)(4,1)S(1)} %copy-done.19), kind=kLoop, calls=%fused_computation.36 | loop fusion | flops 12576768 | bytes 12894208 | tf_op jit(solution)/shard_map/while/body/eval_jaxpr/reduce_sum | solution.py:77
  113.4 20.8 %fusion.36 = f32[12,64,512]{2,1,0:T(8,128)} fusion(bf16[512,12,64]{0,2,1:T(8,128)(2,1)} %bitcast.324, f32[12,512,512]{1,2,0:T(8,128)} %get-tuple-element.247, f32[12,512]{1,0:T(8,128)S(1)} %get-tuple-element.210, pred[512,512]{0,1:T(8,128)(4,1)} %get-tuple-element.241), kind=kOutput, calls=%fused_computation.57 | convolution fusion | flops 415236096 | bytes 15228928 | tf_op jit(solution)/shard_map/while/body/eval_jaxpr/hqk,khd->qhd/dot_general | solution.py:78
  142.5 7.3 %fusion.15 = f32[12,512]{1,0:T(8,128)S(1)} fusion(f32[12,512,512]{1,2,0:T(8,128)} %get-tuple-element.245, f32[12,512]{1,0:T(8,128)} %get-tuple-element.196, pred[512,512]{0,1:T(8,128)(4,1)} %get-tuple-element.240), kind=kLoop, calls=%fused_computation.38 | loop fusion | flops 12576768 | bytes 12894208 | tf_op jit(solution)/shard_map/while/body/eval_jaxpr/reduce_sum | solution.py:77
  150.0 8.8 %fusion.158 = (bf16[512,12,64]{0,2,1:T(8,128)(2,1)S(1)}, f32[512,12,64]{0,2,1:T(8,128)}) fusion(f32[512,12]{0,1:T(8,128)S(1)} %get-tuple-element.194, bf16[512,12,64]{0,2,1:T(8,128)(2,1)S(1)} %bitcast.326, f32[12,512,512]{1,2,0:T(8,128)} %get-tuple-element.245, f32[12,512]{1,0:T(8,128)S(1)} %copy-done.37, pred[512,512]{0,1:T(8,128)(4,1)S(1)} %copy-done.21, ...), kind=kOutput, calls=%fused_computation.216 | convolution fusion | flops 417988608 | bytes 19259392 | tf_op jit(solution)/shard_map/while/body/eval_jaxpr/hqk,khd->qhd/dot_general | solution.py:78
  162.6 7.0 %gather_fusion.2 = bf16[1024,768]{1,0:T(8,128)(2,1)} fusion(bf16[512,768]{1,0:T(8,128)(2,1)} %add_convert_fusion.1, s32[1024]{0:T(1024)} %copy-done.44), kind=kCustom, calls=%fused_computation.2 | custom fusion | bytes 3149824 | tf_op jit(solution)/shard_map/gather | solution.py:206
  173.5 4.9 all-to-all-start
  186.3 28.2 %all-to-all-done = bf16[4,256,768]{2,1,0:T(8,128)(2,1)} async-done(((bf16[4,256,768]{2,1,0:T(8,128)(2,1)}), bf16[4,256,768]{2,1,0:T(8,128)(2,1)}, u32[]{:S(2)}, u32[]{:S(2)}) %all-to-all-start) | async-done | bytes 1572896 | tf_op jit(solution)/shard_map/all_to_all | solution.py:207
  218.9 7.4 %fusion.54 = f32[4,256,3072]{2,1,0:T(8,128)S(1)} fusion(bf16[4,256,768]{2,1,0:T(8,128)(2,1)} %all-to-all-done, bf16[1,768,3072]{2,1,0:T(8,128)(2,1)} %param.23), kind=kOutput, calls=%fused_computation.69 | convolution fusion | flops 4831838208 | bytes 18874368 | tf_op jit(solution)/shard_map/secd,edf->secf/dot_general | solution.py:209
  230.7 10.8 %fusion.77 = bf16[4,256,768]{2,1,0:T(8,128)(2,1)} fusion(bf16[1,3072,768]{2,1,0:T(8,128)(2,1)} %param.24, f32[4,256,3072]{2,1,0:T(8,128)S(1)} %fusion.54), kind=kOutput, calls=%fused_computation.95 | convolution fusion | flops 4860936192 | bytes 18874368 | tf_op jit(solution)/shard_map/secf,efd->secd/dot_general | solution.py:212
  241.5 13.9 %all-to-all-done.2 = bf16[4,256,768]{2,1,0:T(8,128)(2,1)} async-done(((bf16[4,256,768]{2,1,0:T(8,128)(2,1)}), bf16[4,256,768]{2,1,0:T(8,128)(2,1)}, u32[]{:S(2)}, u32[]{:S(2)}) %all-to-all-start.2) | async-done | bytes 1572896 | tf_op jit(solution)/shard_map/all_to_all | solution.py:227
  260.2 15.3 %fusion.6 = bf16[4,1,256,3072]{3,2,0,1:T(8,128)(2,1)S(1)} fusion(f32[4,256,3072]{2,1,0:T(8,128)} %copy-done.64, bf16[4,256,768]{2,1,0:T(8,128)(2,1)} %all-to-all-done.2, bf16[1,3072,768]{2,1,0:T(8,128)(2,1)} %param.24), kind=kOutput, calls=%fused_computation.14 | convolution fusion | flops 4894752768 | bytes 25165824 | tf_op jit(solution)/shard_map/secd,efd->secf/dot_general | solution.py:233
  275.5 8.5 %fusion.82 = bf16[4,256,768]{2,1,0:T(8,128)(2,1)} fusion(bf16[1,768,3072]{2,1,0:T(8,128)(2,1)} %param.23, bf16[4,1,256,3072]{3,2,0,1:T(8,128)(2,1)S(1)} %fusion.6), kind=kOutput, calls=%fused_computation.96 | convolution fusion | flops 4832624640 | bytes 12582912 | tf_op jit(solution)/shard_map/secf,edf->secd/dot_general | solution.py:238
  284.1 8.2 %fusion.56 = bf16[1,768,3072]{2,1,0:T(8,128)(2,1)} fusion(bf16[4,256,768]{2,1,0:T(8,128)(2,1)} %all-to-all-done, bf16[4,1,256,3072]{3,2,0,1:T(8,128)(2,1)S(1)} %fusion.6), kind=kOutput, calls=%fused_computation.71 | convolution fusion | flops 4834197504 | bytes 12582912 | tf_op jit(solution)/shard_map/secd,secf->edf/dot_general | solution.py:237
  301.1 12.0 %fusion.59 = bf16[1,3072,768]{2,1,0:T(8,128)(2,1)} fusion(bf16[4,256,768]{2,1,0:T(8,128)(2,1)} %all-to-all-done.2, f32[4,256,3072]{2,1,0:T(8,128)} %copy-done.64), kind=kOutput, calls=%fused_computation.72 | convolution fusion | flops 4862509056 | bytes 18874368 | tf_op jit(solution)/shard_map/secf,secd->efd/dot_general | solution.py:230
  318.1 19.5 %all-to-all-done.3 = bf16[4,256,768]{2,1,0:T(8,128)(2,1)} async-done(((bf16[4,256,768]{2,1,0:T(8,128)(2,1)}), bf16[4,256,768]{2,1,0:T(8,128)(2,1)}, u32[]{:S(2)}, u32[]{:S(2)}) %all-to-all-start.3) | async-done | bytes 1572896 | tf_op jit(solution)/shard_map/all_to_all | solution.py:241
  356.2 8.6 %fusion.110 = bf16[12,64,512]{2,1,0:T(8,128)(2,1)} fusion(bf16[512,12,64]{0,2,1:T(8,128)(2,1)} %bitcast.311, f32[12,512,512]{1,2,0:T(8,128)} %get-tuple-element.245, f32[12,512]{1,0:T(8,128)} %log_add_fusion, pred[512,512]{0,1:T(8,128)(4,1)} %get-tuple-element.240), kind=kOutput, calls=%fused_computation.132 | convolution fusion | flops 415629312 | bytes 14442496 | tf_op jit(solution)/shard_map/while/body/eval_jaxpr/hqk,qhd->khd/dot_general | solution.py:126
  364.8 7.8 %multiply_convert_fusion = bf16[12,512,512]{1,2,0:T(8,128)(2,1)S(1)} fusion(f32[12,512,512]{1,2,0:T(8,128)} %get-tuple-element.245, f32[12,512]{1,0:T(8,128)S(1)} %bitcast.331, f32[12,512]{1,0:T(8,128)S(1)} %copy-done.47, pred[512,512]{0,1:T(8,128)(4,1)S(1)} %copy-done.22, bf16[512,12,64]{0,2,1:T(8,128)(2,1)S(1)} %bitcast.312, ...), kind=kOutput, calls=%fused_computation.22 | convolution fusion | flops 421527552 | bytes 20758528 | tf_op jit(solution)/shard_map/while/body/eval_jaxpr/qhd,khd->hqk/dot_general | solution.py:96
  372.7 7.6 %multiply_convert_fusion.2 = bf16[12,512,512]{1,2,0:T(8,128)(2,1)S(1)} fusion(f32[12,512,512]{1,2,0:T(8,128)} %get-tuple-element.262, f32[12,512]{1,0:T(8,128)S(1)} %bitcast.332, f32[12,512]{1,0:T(8,128)S(1)} %copy-done.47, pred[512,512]{0,1:T(8,128)(4,1)} %get-tuple-element.239, bf16[512,12,64]{0,2,1:T(8,128)(2,1)S(1)} %bitcast.313, ...), kind=kOutput, calls=%fused_computation.26 | convolution fusion | flops 421527552 | bytes 20758528 | tf_op jit(solution)/shard_map/while/body/eval_jaxpr/qhd,khd->hqk/dot_general | solution.py:96
  385.8 8.0 %multiply_convert_fusion.1 = bf16[12,512,512]{1,2,0:T(8,128)(2,1)S(1)} fusion(f32[12,512,512]{1,2,0:T(8,128)} %get-tuple-element.247, f32[12,512]{1,0:T(8,128)S(1)} %bitcast.333, f32[12,512]{1,0:T(8,128)S(1)} %copy-done.47, pred[512,512]{0,1:T(8,128)(4,1)} %get-tuple-element.241, bf16[512,12,64]{0,2,1:T(8,128)(2,1)S(1)} %bitcast.314, ...), kind=kOutput, calls=%fused_computation.24 | convolution fusion | flops 421527552 | bytes 20758528 | tf_op jit(solution)/shard_map/while/body/eval_jaxpr/qhd,khd->hqk/dot_general | solution.py:96
  404.0 6.1 fusion.30
  423.5 14.7 %collective-permute-done.3 = bf16[512,1536]{0,1:T(8,128)(2,1)} collective-permute-done((bf16[512,1536]{0,1:T(8,128)(2,1)}, bf16[512,1536]{0,1:T(8,128)(2,1)}, u32[]{:S(2)}, u32[]{:S(2)}) %collective-permute-start.3) | collective-permute-done | bytes 1572896 | tf_op jit(solution)/shard_map/ppermute | solution.py:17
  441.4 5.3 fusion.106
  446.7 23.3 %all-reduce.8.cloned.1.call-done = (bf16[1,768,3072]{2,1,0:T(8,128)(2,1)}, bf16[1,3072,768]{2,1,0:T(8,128)(2,1)}) async-done(((bf16[1,768,3072]{2,1,0:T(8,128)(2,1)}, bf16[1,3072,768]{2,1,0:T(8,128)(2,1)}), (bf16[1,768,3072]{2,1,0:T(8,128)(2,1)}, bf16[1,3072,768]{2,1,0:T(8,128)(2,1)})) %all-reduce.8.cloned.1.call-update) | async-done | bytes 9437200 | tf_op jit(solution)/shard_map/psum | solution.py:304
  470.0 7.5 %convert_element_type.162 = f32[1,768,3072]{2,1,0:T(8,128)} convert(bf16[1,768,3072]{2,1,0:T(8,128)(2,1)} %get-tuple-element.192) | non-fusion elementwise | flops 2359296 | bytes 14155776 | tf_op jit(solution)/shard_map/convert_element_type | solution.py:304
  486.2 55.8 %all-reduce = (f32[768]{0:T(1024)}, f32[768]{0:T(1024)}, f32[768]{0:T(1024)}, f32[768]{0:T(1024)}) all-reduce(f32[768]{0:T(1024)} %get-tuple-element.167, f32[768]{0:T(1024)} %get-tuple-element.170, f32[768]{0:T(1024)S(1)} %get-tuple-element.165, f32[768]{0:T(1024)S(1)} %copy-done.50), channel_id=1, replica_groups=mesh['seq'=8,'exp'=4] {'seq','exp'}, use_global_device_ids=true, to_apply=%region_23.24 | all-reduce | flops 3072 | bytes 24576 | tf_op jit(solution)/shard_map/psum | solution.py:292
  547.3 129.1 %all-reduce.6.cloned.1.call-done = (f32[768,2304]{1,0:T(8,128)}, f32[768,768]{1,0:T(8,128)}) async-done(((f32[768,2304]{1,0:T(8,128)}, f32[768,768]{1,0:T(8,128)}), (f32[768,2304]{1,0:T(8,128)}, f32[768,768]{1,0:T(8,128)})) %all-reduce.6.cloned.1.call-update) | async-done | bytes 9437200 | tf_op jit(solution)/shard_map/psum | solution.py:292
  676.4 6.6 copy.132
  (239 shorter events, 172.4 us)
Async XLA Ops:
  10.2 9.6 %copy-start.57 = (s32[1,512]{1,0:T(1,128)S(1)}, s32[1,512]{1,0:T(1,128)}, u32[]{:S(2)}) copy-start(s32[1,512]{1,0:T(1,128)} %param.14) | copy-start | bytes 6148
  16.2 29.7 %collective-permute-start = (bf16[512,1536]{1,0:T(8,128)(2,1)}, bf16[512,1536]{1,0:T(8,128)(2,1)}, u32[]{:S(2)}, u32[]{:S(2)}) collective-permute-start(bf16[512,1536]{1,0:T(8,128)(2,1)} %slice.67), channel_id=1, source_target_pairs={{0,4},{4,8},{8,12},{12,16},{16,20},{20,24},{24,28},{1,5},{5,9},{9,... | collective-permute-start | bytes 4718600 | tf_op jit(solution)/shard_map/ppermute | solution.py:17
  40.5 18.1 %copy-start.44 = (s32[1024]{0:T(1024)}, s32[1024]{0:T(1024)S(1)}, u32[]{:S(2)}) copy-start(s32[1024]{0:T(1024)S(1)} %broadcast_clamp_fusion) | copy-start | bytes 12292
  45.9 44.2 %collective-permute-start.1 = (bf16[512,1536]{1,0:T(8,128)(2,1)}, bf16[512,1536]{1,0:T(8,128)(2,1)}, u32[]{:S(2)}, u32[]{:S(2)}) collective-permute-start(bf16[512,1536]{1,0:T(8,128)(2,1)} %collective-permute-done), channel_id=1, source_target_pairs={{0,4},{4,8},{8,12},{12,16},{16,20},{20,24},{24,28},{1,5},{5,9},{9,... | collective-permute-start | bytes 4718600 | tf_op jit(solution)/shard_map/ppermute | solution.py:17
  97.3 8.8 %copy-start.19 = (pred[512,512]{0,1:T(8,128)(4,1)S(1)}, pred[512,512]{0,1:T(8,128)(4,1)}, u32[]{:S(2)}) copy-start(pred[512,512]{0,1:T(8,128)(4,1)} %get-tuple-element.241) | copy-start | bytes 786436
  106.1 28.1 %slice-start = ((s8[12582912]{0:T(1024)(128)(4,1)}), s8[4194304]{0:T(1024)(128)(4,1)S(1)}, s32[]{:S(2)}) async-start(s8[12582912]{0:T(1024)(128)(4,1)} %bitcast.290), calls=%async_computation.6 | async-start | bytes 8388608
  106.1 28.1 %slice-start.1 = ((s8[12582912]{0:T(1024)(128)(4,1)}), s8[4194304]{0:T(1024)(128)(4,1)S(1)}, s32[]{:S(2)}) async-start(s8[12582912]{0:T(1024)(128)(4,1)} %bitcast.290), calls=%async_computation.7 | async-start | bytes 8388608
  113.4 36.4 %copy-start.34 = (f32[12,512]{1,0:T(8,128)}, f32[12,512]{1,0:T(8,128)S(1)}, u32[]{:S(2)}) copy-start(f32[12,512]{1,0:T(8,128)S(1)} %fusion.13) | copy-start | bytes 73732
  113.4 20.8 %slice-start.2 = ((s8[12582912]{0:T(1024)(128)(4,1)}), s8[4194304]{0:T(1024)(128)(4,1)S(1)}, s32[]{:S(2)}) async-start(s8[12582912]{0:T(1024)(128)(4,1)} %bitcast.290), calls=%async_computation.8 | async-start | bytes 8388608
  137.8 12.1 %copy-start.35 = (f32[12,512]{1,0:T(8,128)}, f32[12,512]{1,0:T(8,128)S(1)}, u32[]{:S(2)}) copy-start(f32[12,512]{1,0:T(8,128)S(1)} %fusion.11) | copy-start | bytes 73732
  149.9 8.9 %copy-start.36 = (f32[12,512]{1,0:T(8,128)}, f32[12,512]{1,0:T(8,128)S(1)}, u32[]{:S(2)}) copy-start(f32[12,512]{1,0:T(8,128)S(1)} %fusion.15) | copy-start | bytes 73732
  150.0 8.8 %copy-start.10 = (bf16[1,512,768]{2,1,0:T(8,128)(2,1)S(1)}, bf16[1,512,768]{2,1,0:T(8,128)(2,1)}, u32[]{:S(2)}) copy-start(bf16[1,512,768]{2,1,0:T(8,128)(2,1)} %param.13) | copy-start | bytes 2359300
  150.0 8.8 %copy-start.59 = (bf16[768,768]{1,0:T(8,128)(2,1)S(1)}, bf16[768,768]{1,0:T(8,128)(2,1)}, u32[]{:S(2)}) copy-start(bf16[768,768]{1,0:T(8,128)(2,1)} %param.22) | copy-start | bytes 3538948
  173.5 41.0 %all-to-all-start = ((bf16[4,256,768]{2,1,0:T(8,128)(2,1)}), bf16[4,256,768]{2,1,0:T(8,128)(2,1)}, u32[]{:S(2)}, u32[]{:S(2)}) async-start(bf16[4,256,768]{2,1,0:T(8,128)(2,1)} %get-tuple-element.243), calls=%async_computation | async-start | bytes 3145728 | tf_op jit(solution)/shard_map/all_to_all | solution.py:207
  214.5 40.9 %all-to-all-start.2 = ((bf16[4,256,768]{2,1,0:T(8,128)(2,1)}), bf16[4,256,768]{2,1,0:T(8,128)(2,1)}, u32[]{:S(2)}, u32[]{:S(2)}) async-start(bf16[4,256,768]{2,1,0:T(8,128)(2,1)} %get-tuple-element.242), calls=%async_computation.2 | async-start | bytes 3145728 | tf_op jit(solution)/shard_map/all_to_all | solution.py:227
  255.4 41.3 %all-to-all-start.1 = ((bf16[4,256,768]{2,1,0:T(8,128)(2,1)}), bf16[4,256,768]{2,1,0:T(8,128)(2,1)}, u32[]{:S(2)}, u32[]{:S(2)}) async-start(bf16[4,256,768]{2,1,0:T(8,128)(2,1)} %fusion.77), calls=%async_computation.1 | async-start | bytes 3145728 | tf_op jit(solution)/shard_map/all_to_all | solution.py:215
  296.7 40.9 %all-to-all-start.3 = ((bf16[4,256,768]{2,1,0:T(8,128)(2,1)}), bf16[4,256,768]{2,1,0:T(8,128)(2,1)}, u32[]{:S(2)}, u32[]{:S(2)}) async-start(bf16[4,256,768]{2,1,0:T(8,128)(2,1)} %fusion.82), calls=%async_computation.3 | async-start | bytes 3145728 | tf_op jit(solution)/shard_map/all_to_all | solution.py:241
  301.1 169.0 %all-reduce.8.cloned.1.call-start = ((), (), s32[]{:S(2)}) async-start(), calls=%async_computation.5 | async-start | bytes 18874368 | tf_op jit(solution)/shard_map/psum | solution.py:304
  313.2 363.2 %all-reduce.6.cloned.1.call-start = ((), (), s32[]{:S(2)}) async-start(), calls=%async_computation.4 | async-start | bytes 18874368 | tf_op jit(solution)/shard_map/psum | solution.py:292
  318.1 24.2 %copy-start.46 = (f32[512]{0:T(512)S(1)}, f32[512]{0:T(512)}, u32[]{:S(2)}) copy-start(f32[512]{0:T(512)} %copy-done.45) | copy-start | bytes 6148
  356.2 8.6 %copy-start.17 = (bf16[512,768]{0,1:T(8,128)(2,1)S(1)}, bf16[512,768]{0,1:T(8,128)(2,1)}, u32[]{:S(2)}) copy-start(bf16[512,768]{0,1:T(8,128)(2,1)} %copy.94) | copy-start | bytes 2359300
  397.1 13.0 %collective-permute-start.2 = (bf16[512,1536]{0,1:T(8,128)(2,1)}, bf16[512,1536]{0,1:T(8,128)(2,1)}, u32[]{:S(2)}, u32[]{:S(2)}) collective-permute-start(bf16[512,1536]{0,1:T(8,128)(2,1)} %pad_maximum_fusion.1), channel_id=1, source_target_pairs={{4,0},{8,4},{12,8},{16,12},{20,16},{24,20},{28,24},{5,1},{9,5},{13... | collective-permute-start | bytes 4718600 | tf_op jit(solution)/shard_map/ppermute | solution.py:17
  404.0 15.7 %slice-start.3 = ((s8[12582912]{0:T(1024)(128)(4,1)}), s8[4194304]{0:T(1024)(128)(4,1)S(1)}, s32[]{:S(2)}) async-start(s8[12582912]{0:T(1024)(128)(4,1)} %bitcast.292), calls=%async_computation.9 | async-start | bytes 8388608
  404.0 15.7 %slice-start.4 = ((s8[12582912]{0:T(1024)(128)(4,1)}), s8[4194304]{0:T(1024)(128)(4,1)S(1)}, s32[]{:S(2)}) async-start(s8[12582912]{0:T(1024)(128)(4,1)} %bitcast.292), calls=%async_computation.10 | async-start | bytes 8388608
  413.6 24.5 %collective-permute-start.3 = (bf16[512,1536]{0,1:T(8,128)(2,1)}, bf16[512,1536]{0,1:T(8,128)(2,1)}, u32[]{:S(2)}, u32[]{:S(2)}) collective-permute-start(bf16[512,1536]{0,1:T(8,128)(2,1)} %fusion.64), channel_id=1, source_target_pairs={{4,0},{8,4},{12,8},{16,12},{20,16},{24,20},{28,24},{5,1},{9,5},{13... | collective-permute-start | bytes 4718600 | tf_op jit(solution)/shard_map/ppermute | solution.py:17
  419.8 18.4 %copy-start.14 = (f32[12,64,512]{2,1,0:T(8,128)S(1)}, f32[12,64,512]{2,1,0:T(8,128)}, u32[]{:S(2)}) copy-start(f32[12,64,512]{2,1,0:T(8,128)} %convolution_multiply_fusion) | copy-start | bytes 4718596
  423.4 17.9 %copy-start.11 = (bf16[1,512,768]{2,1,0:T(8,128)(2,1)S(1)}, bf16[1,512,768]{2,1,0:T(8,128)(2,1)}, u32[]{:S(2)}) copy-start(bf16[1,512,768]{2,1,0:T(8,128)(2,1)} %param.13) | copy-start | bytes 2359300
  423.4 17.9 %copy-start.31 = (bf16[12,64,512]{2,1,0:T(8,128)(2,1)S(1)}, bf16[12,64,512]{2,1,0:T(8,128)(2,1)}, u32[]{:S(2)}) copy-start(bf16[12,64,512]{2,1,0:T(8,128)(2,1)} %multiply_convert_fusion.4) | copy-start | bytes 2359300
  423.4 17.9 %copy-start.49 = (f32[512]{0:T(512)S(1)}, f32[512]{0:T(512)}, u32[]{:S(2)}) copy-start(f32[512]{0:T(512)} %copy-done.48) | copy-start | bytes 6148
  423.4 17.9 %copy-start.52 = (f32[512]{0:T(512)S(1)}, f32[512]{0:T(512)}, u32[]{:S(2)}) copy-start(f32[512]{0:T(512)} %copy-done.51) | copy-start | bytes 6148
  423.4 17.9 %copy-start.54 = (f32[768]{0:T(1024)S(1)}, f32[768]{0:T(1024)}, u32[]{:S(2)}) copy-start(f32[768]{0:T(1024)} %param.17) | copy-start | bytes 9220
  423.4 17.9 %copy-start.61 = (f32[768]{0:T(1024)S(1)}, f32[768]{0:T(1024)}, u32[]{:S(2)}) copy-start(f32[768]{0:T(1024)} %param.18) | copy-start | bytes 9220
  (49 other events, 252.8 us)
Sparse Core Ops, SparseCore 0:
  313.3 156.6 all-reduce.7
  477.5 198.8 all-reduce.5
where the time goes:
time: 699 us; the launch traced here: 692 us
  waiting for transfers between devices  233 us (33%)
  matrix products  196 us (28%)
  local copies, waits for them, and re-layouts  86.4 us (12%)
  other arithmetic  74.9 us (11%)
  blocking collectives  55.8 us (8%)
  starting transfers between devices  29.9 us (4%)
  between operations  15.3 us (2%)
    psum x1, waiting for transfers between devices, on_device(): lax.psum((grad_w_qkv, grad_w_out, grad_first_gain, grad_first_bias, grad_...  129 us
    psum x1, blocking collectives, on_device(): lax.psum((grad_w_qkv, grad_w_out, grad_first_gain, grad_first_bias, grad_...  55.8 us
    dot_general x3, matrix products, step(): jnp.einsum('hqk,khd->qhd', shares.astype(jnp.bfloat16), value_rows, prefe...  34.3 us
    all_to_all x1, waiting for transfers between devices, on_device(): lax.all_to_all(send, 'exp', split_axis=0, concat_axis=0, tiled=True)  28.2 us
    dot_general x3, matrix products, step(): jnp.einsum('qhd,khd->hqk', queries, key_rows, preferred_element_type=jnp....  25.3 us
    dot_general x3, matrix products, backward_core(): jnp.einsum('qhd,khd->hqk', grad_heads, value_rows, preferred_element_type...  23.4 us
    psum x1, waiting for transfers between devices, on_device(): lax.psum(grad_w_up.astype(jnp.bfloat16), 'seq').astype(jnp.float32)  23.3 us
    all_to_all x1, waiting for transfers between devices, on_device(): lax.all_to_all(grad_slots.reshape(experts_total, capacity, width), 'exp',...  19.5 us
  transfers between devices with their start and end apart: 10, of which 7 were waited for; matrix products, arithmetic and copies ran while one was open for 36% of the time, Pallas kernels for 0%

commit v1 on v0

--- a/solution.py
+++ b/solution.py
@@ -289,17 +289,16 @@
     grad_first_gain = jnp.sum(grad_attn_in * normed_one, axis=0)
     grad_first_bias = jnp.sum(grad_attn_in, axis=0)
     grad_input = grad_resid + norm_back(grad_attn_in * first_gain, normed_one, scale_one)
-    dense = lax.psum(
-        (
-            grad_w_qkv,
-            grad_w_out,
-            grad_first_gain,
-            grad_first_bias,
-            grad_second_gain,
-            grad_second_bias,
-        ),
-        ("seq", "exp"),
-    )
+    dense = (
+        grad_w_qkv,
+        grad_w_out,
+        grad_first_gain,
+        grad_first_bias,
+        grad_second_gain,
+        grad_second_bias,
+    )
+    for over in ("exp", "seq"):
+        dense = lax.psum(dense, over)
     expert_sums = (
         lax.psum(grad_w_up.astype(jnp.bfloat16), "seq").astype(jnp.float32),
         lax.psum(grad_w_down.astype(jnp.bfloat16), "seq").astype(jnp.float32),

time: 699 us -> 1060 us (1.52)
  waiting for transfers between devices: 233 us -> 591 us
  blocking collectives: 55.8 us -> 84.3 us
  matrix products: 196 us -> 183 us
    psum x1 -> x2, waiting for transfers between devices: 129 us -> 397 us  [on_device(): dense = lax.psum(dense, over)]
    psum x1, waiting for transfers between devices: 23.3 us -> 142 us  [on_device(): lax.psum(grad_w_up.astype(jnp.bfloat16), 'seq').astype(jnp.float32)]
    all_to_all x0 -> x1, blocking collectives: none -> 40.7 us  [on_device(): lax.all_to_all(send, 'exp', split_axis=0, concat_axis=0, tiled=True)]
    all_to_all x1 -> x0, waiting for transfers between devices: 28.2 us -> none  [on_device(): lax.all_to_all(send, 'exp', split_axis=0, concat_axis=0, tiled=True)]
    psum x1 -> x2, blocking collectives: 55.8 us -> 43.6 us  [on_device(): dense = lax.psum(dense, over)]
    dot_general x3, matrix products: 34.3 us -> 22.4 us  [step(): jnp.einsum('hqk,khd->qhd', shares.astype(jnp.bfloat16), value_rows, prefe...]
  transfers between devices with their start and end apart: 10 -> 10, of which waited for: 7 -> 7; matrix products, arithmetic and copies ran while one was open for 36% -> 17% of each run, Pallas kernels for 0% -> 0%
where the time goes in v1:
time: 1060 us
  waiting for transfers between devices  591 us (56%)
  matrix products  183 us (17%)
  local copies, waits for them, and re-layouts  84.3 us (8%)
  blocking collectives  84.3 us (8%)
  other arithmetic  74.7 us (7%)
  starting transfers between devices  24.4 us (2%)
  between operations  14.8 us (1%)
    psum x2, waiting for transfers between devices, on_device(): dense = lax.psum(dense, over)  397 us
    psum x1, waiting for transfers between devices, on_device(): lax.psum(grad_w_up.astype(jnp.bfloat16), 'seq').astype(jnp.float32)  142 us
    psum x2, blocking collectives, on_device(): dense = lax.psum(dense, over)  43.6 us
    all_to_all x1, blocking collectives, on_device(): lax.all_to_all(send, 'exp', split_axis=0, concat_axis=0, tiled=True)  40.7 us
    dot_general x3, matrix products, step(): jnp.einsum('qhd,khd->hqk', queries, key_rows, preferred_element_type=jnp....  25.3 us
    all_to_all x1, waiting for transfers between devices, on_device(): lax.all_to_all(grad_slots.reshape(experts_total, capacity, width), 'exp',...  23.4 us
    dot_general x3, matrix products, step(): jnp.einsum('hqk,khd->qhd', shares.astype(jnp.bfloat16), value_rows, prefe...  22.4 us
    dot_general x3, matrix products, backward_core(): jnp.einsum('qhd,khd->hqk', grad_heads, value_rows, preferred_element_type...  21.7 us
  transfers between devices with their start and end apart: 10, of which 7 were waited for; matrix products, arithmetic and copies ran while one was open for 17% of the time, Pallas kernels for 0%

profile of v1, /device:TPU:0, one launch (start us, length us, event | category | flops | bytes accessed | tf_op | source)
XLA Modules:
  0.0 1056.4 jit_solution(16201259911674707032)
XLA Ops:
  27.7 6.9 gather_fusion.1
  53.5 7.0 gather_fusion.4
  60.5 8.6 select_reduce_fusion.2
  76.3 8.7 select_reduce_fusion.1
  92.2 8.0 select_reduce_fusion
  100.9 7.3 fusion.13
  108.2 8.9 fusion.36
  125.4 7.3 fusion.15
  132.8 8.8 fusion.158
  145.5 7.0 gather_fusion.2
  155.9 40.7 %all_to_all.20 = bf16[4,256,768]{2,1,0:T(8,128)(2,1)} all-to-all(bf16[4,256,768]{2,1,0:T(8,128)(2,1)S(1)} %get-tuple-element.262), channel_id=1, replica_groups=mesh['seq'=8,'exp'=4] {'exp'}, dimensions={0} | all-to-all | bytes 3145728 | tf_op jit(solution)/shard_map/all_to_all | solution.py:207
  200.9 7.4 fusion.54
  212.8 10.7 %fusion.77 = bf16[4,256,768]{2,1,0:T(8,128)(2,1)} fusion(bf16[1,3072,768]{2,1,0:T(8,128)(2,1)} %param.24, f32[4,256,3072]{2,1,0:T(8,128)S(1)} %fusion.54), kind=kOutput, calls=%fused_computation.95 | convolution fusion | flops 4860936192 | bytes 18874368 | tf_op jit(solution)/shard_map/secf,efd->secd/dot_general | solution.py:212
  223.5 13.5 %all-to-all-done.2 = bf16[4,256,768]{2,1,0:T(8,128)(2,1)} async-done(((bf16[4,256,768]{2,1,0:T(8,128)(2,1)}), bf16[4,256,768]{2,1,0:T(8,128)(2,1)}, u32[]{:S(2)}, u32[]{:S(2)}) %all-to-all-start.2) | async-done | bytes 1572896 | tf_op jit(solution)/shard_map/all_to_all | solution.py:227
  241.5 15.3 %fusion.6 = bf16[4,1,256,3072]{3,2,0,1:T(8,128)(2,1)S(1)} fusion(f32[4,256,3072]{2,1,0:T(8,128)} %copy-done.65, bf16[4,256,768]{2,1,0:T(8,128)(2,1)} %all-to-all-done.2, bf16[1,3072,768]{2,1,0:T(8,128)(2,1)} %param.24), kind=kOutput, calls=%fused_computation.14 | convolution fusion | flops 4894752768 | bytes 25165824 | tf_op jit(solution)/shard_map/secd,efd->secf/dot_general | solution.py:233
  259.5 8.5 fusion.82
  268.1 9.9 all-to-all-done.1
  295.5 23.4 %all-to-all-done.3 = bf16[4,256,768]{2,1,0:T(8,128)(2,1)} async-done(((bf16[4,256,768]{2,1,0:T(8,128)(2,1)}), bf16[4,256,768]{2,1,0:T(8,128)(2,1)}, u32[]{:S(2)}, u32[]{:S(2)}) %all-to-all-start.3) | async-done | bytes 1572896 | tf_op jit(solution)/shard_map/all_to_all | solution.py:241
  337.3 8.3 fusion.110
  345.6 7.0 multiply_convert_fusion
  352.7 7.5 multiply_convert_fusion.2
  365.7 7.2 multiply_convert_fusion.1
  383.1 6.1 fusion.30
  416.2 9.1 fusion.56
  425.3 12.1 %fusion.59 = bf16[1,3072,768]{2,1,0:T(8,128)(2,1)} fusion(bf16[4,256,768]{2,1,0:T(8,128)(2,1)} %all-to-all-done.2, f32[4,256,3072]{2,1,0:T(8,128)} %copy-done.65), kind=kOutput, calls=%fused_computation.72 | convolution fusion | flops 4862509056 | bytes 18874368 | tf_op jit(solution)/shard_map/secf,secd->efd/dot_general | solution.py:230
  437.4 319.7 %all-reduce.11.cloned.1.call-done = (f32[768,2304]{1,0:T(8,128)}, f32[768,768]{1,0:T(8,128)}) async-done(((f32[768,2304]{1,0:T(8,128)}, f32[768,768]{1,0:T(8,128)}), (f32[768,2304]{1,0:T(8,128)}, f32[768,768]{1,0:T(8,128)})) %all-reduce.11.cloned.1.call-update) | async-done | bytes 9437200 | tf_op jit(solution)/shard_map/psum | solution.py:301
  757.1 141.6 %all-reduce.13.cloned.1.call-done = (bf16[1,768,3072]{2,1,0:T(8,128)(2,1)}, bf16[1,3072,768]{2,1,0:T(8,128)(2,1)}) async-done(((bf16[1,768,3072]{2,1,0:T(8,128)(2,1)}, bf16[1,3072,768]{2,1,0:T(8,128)(2,1)}), (bf16[1,768,3072]{2,1,0:T(8,128)(2,1)}, bf16[1,3072,768]{2,1,0:T(8,128)(2,1)})) %all-reduce.13.cloned.1.call-update) | async-done | bytes 9437200 | tf_op jit(solution)/shard_map/psum | solution.py:303
  898.7 7.5 convert_element_type.162
  915.3 19.4 %all-reduce.2 = (f32[768]{0:T(1024)}, f32[768]{0:T(1024)}, f32[768]{0:T(1024)}, f32[768]{0:T(1024)}) all-reduce(f32[768]{0:T(1024)} %get-tuple-element.167, f32[768]{0:T(1024)} %get-tuple-element.170, f32[768]{0:T(1024)S(1)} %get-tuple-element.165, f32[768]{0:T(1024)S(1)} %copy-done.50), channel_id=1, replica_groups=mesh['seq'=8,'exp'=4] {'exp'}, use_global_device_ids=true, to_apply=%region_25.26 | all-reduce | flops 3072 | bytes 24576 | tf_op jit(solution)/shard_map/psum | solution.py:301
  934.6 24.3 %all-reduce = (f32[768]{0:T(1024)}, f32[768]{0:T(1024)}, f32[768]{0:T(1024)}, f32[768]{0:T(1024)}) all-reduce(f32[768]{0:T(1024)} %get-tuple-element.192, f32[768]{0:T(1024)} %get-tuple-element.193, f32[768]{0:T(1024)} %get-tuple-element.194, f32[768]{0:T(1024)} %get-tuple-element.195), channel_id=1, replica_groups=mesh['seq'=8,'exp'=4] {'seq'}, use_global_device_ids=true, to_apply=%region_26.27 | all-reduce | flops 3072 | bytes 24576 | tf_op jit(solution)/shard_map/psum | solution.py:301
  964.1 77.6 %all-reduce.9.cloned.1.call-done = (f32[768,2304]{1,0:T(8,128)}, f32[768,768]{1,0:T(8,128)}) async-done(((f32[768,2304]{1,0:T(8,128)}, f32[768,768]{1,0:T(8,128)}), (f32[768,2304]{1,0:T(8,128)}, f32[768,768]{1,0:T(8,128)})) %all-reduce.9.cloned.1.call-update) | async-done | bytes 9437200 | tf_op jit(solution)/shard_map/psum | solution.py:301
  1041.6 6.6 copy.134
  (244 shorter events, 179.9 us)
Async XLA Ops:
  10.2 9.5 copy-start.57
  16.2 24.5 %collective-permute-start = (bf16[512,1536]{1,0:T(8,128)(2,1)}, bf16[512,1536]{1,0:T(8,128)(2,1)}, u32[]{:S(2)}, u32[]{:S(2)}) collective-permute-start(bf16[512,1536]{1,0:T(8,128)(2,1)} %slice.67), channel_id=1, source_target_pairs={{0,4},{4,8},{8,12},{12,16},{16,20},{20,24},{24,28},{1,5},{5,9},{9,... | collective-permute-start | bytes 4718600 | tf_op jit(solution)/shard_map/ppermute | solution.py:17
  35.4 18.1 %copy-start.44 = (s32[1024]{0:T(1024)}, s32[1024]{0:T(1024)S(1)}, u32[]{:S(2)}) copy-start(s32[1024]{0:T(1024)S(1)} %broadcast_clamp_fusion) | copy-start | bytes 12292
  40.7 44.3 %collective-permute-start.1 = (bf16[512,1536]{1,0:T(8,128)(2,1)}, bf16[512,1536]{1,0:T(8,128)(2,1)}, u32[]{:S(2)}, u32[]{:S(2)}) collective-permute-start(bf16[512,1536]{1,0:T(8,128)(2,1)} %collective-permute-done), channel_id=1, source_target_pairs={{0,4},{4,8},{8,12},{12,16},{16,20},{20,24},{24,28},{1,5},{5,9},{9,... | collective-permute-start | bytes 4718600 | tf_op jit(solution)/shard_map/ppermute | solution.py:17
  92.2 8.6 copy-start.19
  100.8 16.3 %slice-start = ((s8[12582912]{0:T(1024)(128)(4,1)}), s8[4194304]{0:T(1024)(128)(4,1)S(1)}, s32[]{:S(2)}) async-start(s8[12582912]{0:T(1024)(128)(4,1)} %bitcast.290), calls=%async_computation.7 | async-start | bytes 8388608
  100.8 16.3 %slice-start.1 = ((s8[12582912]{0:T(1024)(128)(4,1)}), s8[4194304]{0:T(1024)(128)(4,1)S(1)}, s32[]{:S(2)}) async-start(s8[12582912]{0:T(1024)(128)(4,1)} %bitcast.290), calls=%async_computation.8 | async-start | bytes 8388608
  108.2 24.5 %copy-start.34 = (f32[12,512]{1,0:T(8,128)}, f32[12,512]{1,0:T(8,128)S(1)}, u32[]{:S(2)}) copy-start(f32[12,512]{1,0:T(8,128)S(1)} %fusion.13) | copy-start | bytes 73732
  108.2 9.0 slice-start.2
  120.7 12.0 %copy-start.35 = (f32[12,512]{1,0:T(8,128)}, f32[12,512]{1,0:T(8,128)S(1)}, u32[]{:S(2)}) copy-start(f32[12,512]{1,0:T(8,128)S(1)} %fusion.11) | copy-start | bytes 73732
  132.7 8.9 copy-start.36
  132.8 8.8 copy-start.10
  132.8 8.8 copy-start.59
  196.6 40.5 %all-to-all-start.2 = ((bf16[4,256,768]{2,1,0:T(8,128)(2,1)}), bf16[4,256,768]{2,1,0:T(8,128)(2,1)}, u32[]{:S(2)}, u32[]{:S(2)}) async-start(bf16[4,256,768]{2,1,0:T(8,128)(2,1)} %get-tuple-element.248), calls=%async_computation.2 | async-start | bytes 3145728 | tf_op jit(solution)/shard_map/all_to_all | solution.py:227
  237.1 40.9 %all-to-all-start.1 = ((bf16[4,256,768]{2,1,0:T(8,128)(2,1)}), bf16[4,256,768]{2,1,0:T(8,128)(2,1)}, u32[]{:S(2)}, u32[]{:S(2)}) async-start(bf16[4,256,768]{2,1,0:T(8,128)(2,1)} %fusion.77), calls=%async_computation.1 | async-start | bytes 3145728 | tf_op jit(solution)/shard_map/all_to_all | solution.py:215
  278.0 40.9 %all-to-all-start.3 = ((bf16[4,256,768]{2,1,0:T(8,128)(2,1)}), bf16[4,256,768]{2,1,0:T(8,128)(2,1)}, u32[]{:S(2)}, u32[]{:S(2)}) async-start(bf16[4,256,768]{2,1,0:T(8,128)(2,1)} %fusion.82), calls=%async_computation.3 | async-start | bytes 3145728 | tf_op jit(solution)/shard_map/all_to_all | solution.py:241
  282.3 474.7 %all-reduce.11.cloned.1.call-start = ((), (), s32[]{:S(2)}) async-start(), calls=%async_computation.5 | async-start | bytes 18874368 | tf_op jit(solution)/shard_map/psum | solution.py:301
  295.5 28.1 %copy-start.46 = (f32[512]{0:T(512)S(1)}, f32[512]{0:T(512)}, u32[]{:S(2)}) copy-start(f32[512]{0:T(512)} %copy-done.45) | copy-start | bytes 6148
  337.3 8.3 copy-start.17
  337.3 8.3 copy-start.22
  337.3 8.3 copy-start.29
  337.3 8.3 copy-start.47
  376.1 13.1 %collective-permute-start.2 = (bf16[512,1536]{0,1:T(8,128)(2,1)}, bf16[512,1536]{0,1:T(8,128)(2,1)}, u32[]{:S(2)}, u32[]{:S(2)}) collective-permute-start(bf16[512,1536]{0,1:T(8,128)(2,1)} %pad_maximum_fusion.1), channel_id=1, source_target_pairs={{4,0},{8,4},{12,8},{16,12},{20,16},{24,20},{28,24},{5,1},{9,5},{13... | collective-permute-start | bytes 4718600 | tf_op jit(solution)/shard_map/ppermute | solution.py:17
  383.1 15.6 %slice-start.3 = ((s8[12582912]{0:T(1024)(128)(4,1)}), s8[4194304]{0:T(1024)(128)(4,1)S(1)}, s32[]{:S(2)}) async-start(s8[12582912]{0:T(1024)(128)(4,1)} %bitcast.292), calls=%async_computation.10 | async-start | bytes 8388608
  383.1 15.6 %slice-start.4 = ((s8[12582912]{0:T(1024)(128)(4,1)}), s8[4194304]{0:T(1024)(128)(4,1)S(1)}, s32[]{:S(2)}) async-start(s8[12582912]{0:T(1024)(128)(4,1)} %bitcast.292), calls=%async_computation.11 | async-start | bytes 8388608
  392.8 14.5 %collective-permute-start.3 = (bf16[512,1536]{0,1:T(8,128)(2,1)}, bf16[512,1536]{0,1:T(8,128)(2,1)}, u32[]{:S(2)}, u32[]{:S(2)}) collective-permute-start(bf16[512,1536]{0,1:T(8,128)(2,1)} %fusion.64), channel_id=1, source_target_pairs={{4,0},{8,4},{12,8},{16,12},{20,16},{24,20},{28,24},{5,1},{9,5},{13... | collective-permute-start | bytes 4718600 | tf_op jit(solution)/shard_map/ppermute | solution.py:17
  398.7 8.7 copy-start.14
  402.4 8.1 copy-start.11
  402.4 8.1 copy-start.31
  402.5 8.1 copy-start.49
  415.9 482.7 %all-reduce.13.cloned.1.call-start = ((), (), s32[]{:S(2)}) async-start(), calls=%async_computation.6 | async-start | bytes 18874368 | tf_op jit(solution)/shard_map/psum | solution.py:303
  437.4 604.3 %all-reduce.9.cloned.1.call-start = ((), (), s32[]{:S(2)}) async-start(), calls=%async_computation.4 | async-start | bytes 18874368 | tf_op jit(solution)/shard_map/psum | solution.py:301
  (50 other events, 254.2 us)
Sparse Core Ops, SparseCore 0:
  416.1 340.9 all-reduce.10
  761.4 137.2 all-reduce.12
  902.9 138.7 all-reduce.8
